TPU v7x, 32 devices: a whole 2x2x4 slice. The times are simulated.
32 devices in a mesh: member: 16 (over z, y, x), domain: 1, group: 2 (over core).
Axes of the slice: x: 2, y: 2, z: 4, core: 2. Of those that a mesh axis runs over, the one named last changes fastest.
Arguments:
- ensemble: float32 [128, 3, 8, 512], P(('member', 'group'), None, 'domain'), may hold values from -1 to 1
- obs_cell: int32 [1, 32, 128], P('domain', ('member', 'group')), may hold values from 0 to 383
- obs_value: float32 [1, 32, 128], P('domain', ('member', 'group')), may hold values from -1.5 to 1.5
- obs_rinv: float32 [1, 32, 128], P('domain', ('member', 'group')), may hold values from 100 to 1600
- obs_live: int32 [1, 32, 128], P('domain', ('member', 'group')), may hold values 0 or 1
Outputs:
- analysed: float32 [128, 3, 8, 512], P(('member', 'group'), None, 'domain')
All inputs are finite; a program needn't handle non-finite values. Where the computation divides by a largest or mean magnitude, that divisor is 1e-20 or more. No bound on the sum of `obs_live` on one device may be relied on, other than what follows from the above.
Results may differ from a plain program's by a relative error of at most 0.00017.
Values sent between devices are 32-bit elements; how exact they have to be, the bound alone decides.
A program may use at most 64 MiB of HBM per device.

v0:
```python
import math

import jax
import jax.numpy as jnp
from jax import lax
from jax.sharding import PartitionSpec as P

PCOL = 16
STEPS = 8
DEEP = 4
NS_ITERS = 5


HIGH = lax.Precision.HIGHEST


def with_halo(block, sides, width):
    for axis, dim in sides:
        count = lax.axis_size(axis)
        forward = [(i, i + 1) for i in range(count - 1)]
        backward = [(target, source) for source, target in forward]
        low = lax.ppermute(
            lax.slice_in_dim(block, block.shape[dim] - width, None, axis=dim), axis, forward
        )
        high = lax.ppermute(lax.slice_in_dim(block, 0, width, axis=dim), axis, backward)
        block = jnp.concatenate([low, block, high], axis=dim)
    return block


def split_parts(values):
    centre = values[:, 1:-1]
    north = values[:, 2:]
    south = values[:, :-2]
    east = jnp.roll(centre, -1, axis=-1)
    west = jnp.roll(centre, 1, axis=-1)
    return (
        0.25 * (north + south + east + west),
        0.5 * (east - west),
        0.5 * (north - south),
        centre,
    )


def advance(padded):
    height = padded[:, 0]
    speed_u = padded[:, 1]
    speed_v = padded[:, 2]
    depth = 1.0 + height
    h_avg, h_dx, h_dy, h_mid = split_parts(height)
    u_avg, u_dx, u_dy, u_mid = split_parts(speed_u)
    v_avg, v_dx, v_dy, v_mid = split_parts(speed_v)
    flux_x = split_parts(depth * speed_u)[1]
    flux_y = split_parts(depth * speed_v)[2]
    new_h = h_avg - 0.3 * (flux_x + flux_y)
    new_u = u_avg - 0.3 * (u_mid * u_dx + v_mid * u_dy + h_dx - 0.2 * v_mid)
    new_v = v_avg - 0.3 * (u_mid * v_dx + v_mid * v_dy + h_dy + 0.2 * u_mid)
    return jnp.stack([new_h, new_u, new_v], axis=1)


def local(ensemble, obs_cell, obs_value, obs_rinv, obs_live):
    physical_fields_vector = ensemble
    mem_local = physical_fields_vector.shape[0]
    rows = physical_fields_vector.shape[2]
    width_x = physical_fields_vector.shape[3]
    strip = lax.axis_index("domain")
    total_rows = rows * lax.axis_size("domain")
    for block_index in range(STEPS // DEEP):
        padded = with_halo(physical_fields_vector, (("domain", 2),), DEEP)
        for sub_index in range(DEEP):
            padded = advance(padded)
            if sub_index + 1 < DEEP:
                margin = DEEP - 1 - sub_index
                global_row = strip * rows - margin + jnp.arange(padded.shape[2])
                inside = (global_row >= 0) & (global_row < total_rows)
                padded = jnp.where(inside[None, None, :, None], padded, 0.0)
        physical_fields_vector = padded
    domain_pieces = width_x // PCOL
    cells = 3 * rows * PCOL
    pieces = (
        physical_fields_vector.reshape(mem_local, 3, rows, domain_pieces, PCOL)
        .transpose(0, 3, 1, 2, 4)
        .reshape(mem_local, domain_pieces, cells)
    )
    gathered = lax.all_to_all(pieces, ("member", "group"), split_axis=1, concat_axis=0, tiled=True)
    members = gathered.reshape(-1, cells)
    ensemble_size = members.shape[0]
    centre_row = jnp.mean(members, axis=0)
    anomaly = members - centre_row
    picker = (obs_cell[0, 0][None, :] == jnp.arange(cells)[:, None]).astype(jnp.float32)
    seen = jnp.dot(anomaly, picker, precision=HIGH)
    seen_mean = jnp.dot(centre_row[None, :], picker, precision=HIGH)[0]
    innov = obs_value[0, 0] - seen_mean
    weight = obs_rinv[0, 0] * obs_live[0, 0].astype(jnp.float32)
    obs_row = (obs_cell[0, 0] % (rows * PCOL) // PCOL).astype(jnp.float32)
    packed = jnp.concatenate([seen, innov[None, :], weight[None, :], obs_row[None, :]], axis=0)[
        :, None, :
    ]
    nearby = with_halo(packed, (("domain", 1),), 1)
    slots = packed.shape[2]
    nearby = nearby.reshape(ensemble_size + 3, 3 * slots)
    offset = (jnp.arange(3 * slots) // slots - 1).astype(jnp.float32)
    dist_y = offset * rows + nearby[ensemble_size + 2] - 0.5 * (rows - 1)
    taper = jnp.exp(-0.5 * (dist_y / rows) * (dist_y / rows))
    weights = nearby[ensemble_size + 1] * taper
    seen_all = nearby[:ensemble_size]
    gram = jnp.dot(seen_all * weights[None, :], seen_all.T, precision=HIGH)
    ident = jnp.eye(ensemble_size, dtype=jnp.float32)
    system = (ensemble_size - 1) / 1.1 * ident + gram
    norm_c = jnp.max(jnp.sum(jnp.abs(system), axis=1))
    root_m = system / norm_c
    inverse = ident
    for turn_index in range(NS_ITERS):
        factor = 1.5 * ident - 0.5 * jnp.dot(inverse, root_m, precision=HIGH)
        if turn_index + 1 < NS_ITERS:
            root_m = jnp.dot(root_m, factor, precision=HIGH)
        inverse = jnp.dot(factor, inverse, precision=HIGH)
    inverse = inverse / jnp.sqrt(norm_c)
    pushed = jnp.dot(seen_all, weights * nearby[ensemble_size], precision=HIGH)
    shift_w = jnp.dot(inverse, jnp.dot(inverse, pushed, precision=HIGH), precision=HIGH)
    mixing = math.sqrt(ensemble_size - 1) * inverse + shift_w[:, None]
    result = centre_row + lax.dot_general(mixing, anomaly, (((0,), (0,)), ((), ())), precision=HIGH)
    returned = lax.all_to_all(
        result.reshape(ensemble_size, 1, cells),
        ("member", "group"),
        split_axis=0,
        concat_axis=1,
        tiled=True,
    )
    return (
        returned.reshape(mem_local, domain_pieces, 3, rows, PCOL)
        .transpose(0, 2, 3, 1, 4)
        .reshape(mem_local, 3, rows, width_x)
    )


def solution(mesh):
    return jax.shard_map(
        local,
        mesh=mesh,
        in_specs=(
            P(("member", "group"), None, "domain", None),
            P("domain", ("member", "group"), None),
            P("domain", ("member", "group"), None),
            P("domain", ("member", "group"), None),
            P("domain", ("member", "group"), None),
        ),
        out_specs=P(("member", "group"), None, "domain", None),
        check_vma=False,
    )
```

profile of v0, /device:TPU:0, one launch (start us, length us, event | category | flops | bytes accessed | tf_op | source)
XLA Modules:
  0.0 58.3 jit_solution(14581572922671972636)
XLA Ops:
  0.0 1.1 %fusion.110 = (f32[4,3,4,512]{3,2,1,0:T(4,128)S(1)}, f32[4,3,4,512]{3,2,1,0:T(4,128)S(1)}) fusion(f32[4,3,8,512]{3,2,1,0:T(8,128)} %param.5), kind=kLoop, calls=%fused_computation.281 | loop fusion | bytes 393216 | tf_op jit(solution)/shard_map/slice | solution.py:23
  1.1 0.7 %collective-permute-start = (f32[4,3,4,512]{3,2,1,0:T(4,128)S(1)}, f32[4,3,4,512]{3,2,1,0:T(4,128)S(1)}, u32[]{:S(2)}, u32[]{:S(2)}) collective-permute-start(f32[4,3,4,512]{3,2,1,0:T(4,128)S(1)} %get-tuple-element.47), channel_id=1, source_target_pairs={} | collective-permute-start | bytes 294920 | tf_op jit(solution)/shard_map/ppermute | solution.py:22
  1.7 0.7 %collective-permute-start.1 = (f32[4,3,4,512]{3,2,1,0:T(4,128)S(1)}, f32[4,3,4,512]{3,2,1,0:T(4,128)S(1)}, u32[]{:S(2)}, u32[]{:S(2)}) collective-permute-start(f32[4,3,4,512]{3,2,1,0:T(4,128)S(1)} %get-tuple-element.48), channel_id=1, source_target_pairs={} | collective-permute-start | bytes 294920 | tf_op jit(solution)/shard_map/ppermute | solution.py:25
  2.5 1.0 %pad_maximum_fusion = f32[4,3,16,512]{3,2,1,0:T(8,128)S(1)} fusion(f32[4,3,4,512]{3,2,1,0:T(4,128)S(1)} %collective-permute-done.1, f32[4,3,8,512]{3,2,1,0:T(8,128)} %param.5, f32[4,3,4,512]{3,2,1,0:T(4,128)S(1)} %collective-permute-done), kind=kLoop, calls=%fused_computation.22 | loop fusion | flops 196608 | bytes 786432 | tf_op jit(solution)/shard_map/concatenate | solution.py:26
  4.3 0.2 subtract_bitcast_fusion.11
  5.8 0.2 subtract_bitcast_fusion.9
  7.3 0.2 subtract_bitcast_fusion.7
  8.9 0.7 %collective-permute-start.2 = (f32[4,3,4,512]{3,2,0,1:T(4,128)S(1)}, f32[4,3,4,512]{3,2,0,1:T(4,128)S(1)}, u32[]{:S(2)}, u32[]{:S(2)}) collective-permute-start(f32[4,3,4,512]{3,2,0,1:T(4,128)S(1)} %get-tuple-element.45), channel_id=1, source_target_pairs={} | collective-permute-start | bytes 294920 | tf_op jit(solution)/shard_map/ppermute | solution.py:22
  9.6 0.7 %collective-permute-start.3 = (f32[4,3,4,512]{3,2,0,1:T(4,128)S(1)}, f32[4,3,4,512]{3,2,0,1:T(4,128)S(1)}, u32[]{:S(2)}, u32[]{:S(2)}) collective-permute-start(f32[4,3,4,512]{3,2,0,1:T(4,128)S(1)} %get-tuple-element.46), channel_id=1, source_target_pairs={} | collective-permute-start | bytes 294920 | tf_op jit(solution)/shard_map/ppermute | solution.py:25
  11.3 0.2 subtract_bitcast_fusion.5
  12.6 0.2 subtract_bitcast_fusion.2
  12.8 0.2 subtract_bitcast_fusion.3
  14.3 0.2 subtract_bitcast_fusion.1
  15.6 0.2 stack.124
  16.0 0.2 stack.125
  16.3 0.2 stack.126
  16.7 0.5 copy.45
  17.2 0.9 %copy.46 = f32[4,32,384]{2,0,1:T(4,128)} copy(f32[4,32,384]{1,2,0:T(8,128)S(1)} %bitcast.251) | data formatting | bytes 393216 | tf_op jit(solution)/shard_map/reshape | solution.py:82
  18.1 7.3 %all-to-all-start = ((f32[4,32,384]{2,0,1:T(4,128)}), f32[4,32,384]{2,0,1:T(4,128)S(1)}, u32[]{:S(2)}, u32[]{:S(2)}) async-start(f32[4,32,384]{2,0,1:T(4,128)} %copy.46), calls=%async_computation | async-start | bytes 393216 | tf_op jit(solution)/shard_map/all_to_all | solution.py:84
  25.5 8.9 %all-to-all-done = f32[4,32,384]{2,0,1:T(4,128)S(1)} async-done(((f32[4,32,384]{2,0,1:T(4,128)}), f32[4,32,384]{2,0,1:T(4,128)S(1)}, u32[]{:S(2)}, u32[]{:S(2)}) %all-to-all-start) | async-done | bytes 196640 | tf_op jit(solution)/shard_map/all_to_all | solution.py:84
  34.5 0.3 fusion.10
  34.8 0.2 fusion.8
  35.0 0.8 %collective-permute-start.4 = (f32[131,1,128]{2,0,1:T(8,128)S(1)}, f32[131,1,128]{2,0,1:T(8,128)S(1)}, u32[]{:S(2)}, u32[]{:S(2)}) collective-permute-start(f32[131,1,128]{2,0,1:T(8,128)S(1)} %maximum_bitcast_fusion.1), channel_id=1, source_target_pairs={} | collective-permute-start | bytes 201224 | tf_op jit(solution)/shard_map/ppermute | solution.py:22
  35.9 0.4 abs_reduce_fusion
  36.4 0.6 %reduce_max.9 = f32[]{:T(128)} reduce(f32[128]{0:T(128)S(1)} %get-tuple-element.179, f32[]{:T(128)} %constant.138.clone.1), dimensions={0}, to_apply=%region_2.3 | reduce | flops 127 | bytes 520 | tf_op jit(solution)/shard_map/reduce_max | solution.py:109
  37.0 0.8 %fusion.5 = f32[128,128]{0,1:T(8,128)S(1)} fusion(f32[128,128]{0,1:T(8,128)S(1)} %get-tuple-element.180, f32[]{:T(128)} %reduce_max.9), kind=kOutput, calls=%fused_computation.13 | convolution fusion | flops 25264128 | bytes 131076 | tf_op jit(solution)/shard_map/dot_general | solution.py:113
  37.8 0.9 %fusion.54 = f32[128,128]{1,0:T(8,128)S(1)} fusion(f32[128,128]{0,1:T(8,128)S(1)} %fusion.5, f32[128,128]{0,1:T(8,128)S(1)} %get-tuple-element.180, f32[]{:T(128)} %reduce_max.9), kind=kOutput, calls=%fused_computation.202 | convolution fusion | flops 25182208 | bytes 196612 | tf_op jit(solution)/shard_map/dot_general | solution.py:115
  38.8 0.2 fusion.51
  39.0 0.3 fusion.4
  39.3 0.3 fusion.176
  39.6 0.3 fusion.175
  39.9 0.3 fusion.3
  40.2 0.3 fusion.178
  40.4 0.3 fusion.177
  40.7 0.3 fusion.2
  41.0 0.3 fusion.180
  41.3 0.3 fusion.179
  42.4 0.3 fusion.1
  42.7 0.3 convolution_divide_fusion
  43.0 0.3 convolution_bitcast_fusion.3
  43.2 0.2 convolution_bitcast_fusion.2
  43.4 0.2 convolution_bitcast_fusion.1
  43.7 0.5 fusion
  44.2 0.2 copy.55
  44.4 11.4 %all_to_all.30 = f32[128,1,384]{2,1,0:T(1,128)S(1)} all-to-all(f32[128,1,384]{2,1,0:T(1,128)S(1)} %copy.55), channel_id=1, replica_groups=mesh['member'=16,'domain'=1,'group'=2] {'member','group'}, dimensions={0} | all-to-all | bytes 393216 | tf_op jit(solution)/shard_map/all_to_all | solution.py:122
  55.7 0.3 copy.56
  56.0 0.5 copy.57
  56.5 1.7 %reshape.304 = f32[4,3,8,512]{3,2,1,0:T(8,128)} reshape(f32[4,3,8,32,16]{4,3,2,1,0:T(8,128)S(1)} %copy.57) | data formatting | bytes 393216 | tf_op jit(solution)/shard_map/reshape | solution.py:132
  (133 shorter events, 9.8 us)
Async XLA Ops:
  1.1 1.4 %collective-permute-start = (f32[4,3,4,512]{3,2,1,0:T(4,128)S(1)}, f32[4,3,4,512]{3,2,1,0:T(4,128)S(1)}, u32[]{:S(2)}, u32[]{:S(2)}) collective-permute-start(f32[4,3,4,512]{3,2,1,0:T(4,128)S(1)} %get-tuple-element.47), channel_id=1, source_target_pairs={} | collective-permute-start | bytes 294920 | tf_op jit(solution)/shard_map/ppermute | solution.py:22
  1.7 0.7 %collective-permute-start.1 = (f32[4,3,4,512]{3,2,1,0:T(4,128)S(1)}, f32[4,3,4,512]{3,2,1,0:T(4,128)S(1)}, u32[]{:S(2)}, u32[]{:S(2)}) collective-permute-start(f32[4,3,4,512]{3,2,1,0:T(4,128)S(1)} %get-tuple-element.48), channel_id=1, source_target_pairs={} | collective-permute-start | bytes 294920 | tf_op jit(solution)/shard_map/ppermute | solution.py:25
  8.9 1.3 %collective-permute-start.2 = (f32[4,3,4,512]{3,2,0,1:T(4,128)S(1)}, f32[4,3,4,512]{3,2,0,1:T(4,128)S(1)}, u32[]{:S(2)}, u32[]{:S(2)}) collective-permute-start(f32[4,3,4,512]{3,2,0,1:T(4,128)S(1)} %get-tuple-element.45), channel_id=1, source_target_pairs={} | collective-permute-start | bytes 294920 | tf_op jit(solution)/shard_map/ppermute | solution.py:22
  9.6 0.7 %collective-permute-start.3 = (f32[4,3,4,512]{3,2,0,1:T(4,128)S(1)}, f32[4,3,4,512]{3,2,0,1:T(4,128)S(1)}, u32[]{:S(2)}, u32[]{:S(2)}) collective-permute-start(f32[4,3,4,512]{3,2,0,1:T(4,128)S(1)} %get-tuple-element.46), channel_id=1, source_target_pairs={} | collective-permute-start | bytes 294920 | tf_op jit(solution)/shard_map/ppermute | solution.py:25
  16.7 8.8 %copy-start = (s32[1,1,128]{2,1,0:T(1,128)S(1)}, s32[1,1,128]{2,1,0:T(1,128)}, u32[]{:S(2)}) copy-start(s32[1,1,128]{2,1,0:T(1,128)} %param.6) | copy-start | bytes 1540
  16.7 8.8 %copy-start.1 = (f32[1,1,128]{2,1,0:T(1,128)S(1)}, f32[1,1,128]{2,1,0:T(1,128)}, u32[]{:S(2)}) copy-start(f32[1,1,128]{2,1,0:T(1,128)} %param.8) | copy-start | bytes 1540
  16.7 8.8 %copy-start.2 = (s32[1,1,128]{2,1,0:T(1,128)S(1)}, s32[1,1,128]{2,1,0:T(1,128)}, u32[]{:S(2)}) copy-start(s32[1,1,128]{2,1,0:T(1,128)} %param.9) | copy-start | bytes 1540
  17.2 17.6 %copy-start.3 = (f32[1,1,128]{2,1,0:T(1,128)S(1)}, f32[1,1,128]{2,1,0:T(1,128)}, u32[]{:S(2)}) copy-start(f32[1,1,128]{2,1,0:T(1,128)} %param.7) | copy-start | bytes 1540
  18.1 16.3 %all-to-all-start = ((f32[4,32,384]{2,0,1:T(4,128)}), f32[4,32,384]{2,0,1:T(4,128)S(1)}, u32[]{:S(2)}, u32[]{:S(2)}) async-start(f32[4,32,384]{2,0,1:T(4,128)} %copy.46), calls=%async_computation | async-start | bytes 393216 | tf_op jit(solution)/shard_map/all_to_all | solution.py:84
  35.0 0.8 %collective-permute-start.4 = (f32[131,1,128]{2,0,1:T(8,128)S(1)}, f32[131,1,128]{2,0,1:T(8,128)S(1)}, u32[]{:S(2)}, u32[]{:S(2)}) collective-permute-start(f32[131,1,128]{2,0,1:T(8,128)S(1)} %maximum_bitcast_fusion.1), channel_id=1, source_target_pairs={} | collective-permute-start | bytes 201224 | tf_op jit(solution)/shard_map/ppermute | solution.py:22
where the time goes:
time: 58.6 us; the launch traced here: 58.3 us
  local copies, waits for them, and re-layouts  11.8 us (20%)
  blocking collectives  11.4 us (19%)
  starting transfers between devices  10.8 us (18%)
  waiting for transfers between devices  8.9 us (15%)
  matrix products  7.12 us (12%)
  other arithmetic  6.63 us (11%)
  between operations  1.67 us (3%)
    all_to_all x1, blocking collectives, local(): lax.all_to_all(result.reshape(ensemble_size, 1, cells), ('member', 'group...  11.4 us
    all_to_all x1, waiting for transfers between devices, local(): lax.all_to_all(pieces, ('member', 'group'), split_axis=1, concat_axis=0,...  8.89 us
    all_to_all x1, starting transfers between devices, local(): lax.all_to_all(pieces, ('member', 'group'), split_axis=1, concat_axis=0,...  7.33 us
    slice x46, local copies, waits for them, and re-layouts, split_parts(): east = jnp.roll(centre, -1, axis=-1)  4.09 us
    another operation x22, other arithmetic, advance(): return jnp.stack([new_h, new_u, new_v], axis=1)  3.43 us
    ppermute x3, starting transfers between devices, with_halo(): lax.ppermute(lax.slice_in_dim(block, block.shape[dim] - width, None, axis...  2.16 us
    dot_general x5, matrix products, local(): factor = 1.5 * ident - 0.5 * jnp.dot(inverse, root_m, precision=HIGH)  1.99 us
    reshape x1, local copies, waits for them, and re-layouts, local(): return returned.reshape(mem_local, domain_pieces, 3, rows, PCOL).transpos...  1.75 us
  transfers between devices with their start and end apart: 6, of which 1 were waited for; matrix products, arithmetic and copies ran while one was open for 0% of the time, Pallas kernels for 0%

commit v1 on v0

--- a/solution.py
+++ b/solution.py
@@ -1,8 +1,11 @@
+import functools
 import math
 
 import jax
 import jax.numpy as jnp
 from jax import lax
+from jax.experimental import pallas as pl
+from jax.experimental.pallas import tpu as pltpu
 from jax.sharding import PartitionSpec as P
 
 PCOL = 16
@@ -133,9 +136,268 @@
     )
 
 
+def swap_groups(x, row, group):
+    for d in (4, 2, 1):
+        row_bit = (row // d) % 2
+        group_bit = (group // d) % 2
+        up = pltpu.roll(pltpu.roll(x, 8 - d, 0), 16 * d, 1)
+        if d == 4:
+            other = up
+        else:
+            down = pltpu.roll(pltpu.roll(x, d, 0), 128 - 16 * d, 1)
+            other = jnp.where(group_bit == 1, up, down)
+        x = jnp.where(row_bit == group_bit, x, other)
+    return x
+
+
+def swap_members(blocks, row):
+    blocks = list(blocks)
+    for d in (2, 1):
+        low = (row // d) % 2 == 0
+        for i in range(4):
+            if (i // d) % 2 == 0:
+                a, b = blocks[i], blocks[i + d]
+                blocks[i] = jnp.where(low, a, pltpu.roll(b, d, 0))
+                blocks[i + d] = jnp.where(low, pltpu.roll(a, 8 - d, 0), b)
+    return blocks
+
+
+def forecast_step(fields):
+    h, u, v = fields
+    width = h.shape[1]
+    row = lax.broadcasted_iota(jnp.int32, h.shape, 0)
+    first, last = row == 0, row == h.shape[0] - 1
+
+    def around(x):
+        return (
+            pltpu.roll(x, width - 1, 1),
+            pltpu.roll(x, 1, 1),
+            jnp.where(last, 0.0, pltpu.roll(x, x.shape[0] - 1, 0)),
+            jnp.where(first, 0.0, pltpu.roll(x, 1, 0)),
+        )
+
+    he, hw, hn, hs = around(h)
+    ue, uw, un, us = around(u)
+    ve, vw, vn, vs = around(v)
+    flux = ((1.0 + he) * ue - (1.0 + hw) * uw) + ((1.0 + hn) * vn - (1.0 + hs) * vs)
+    new_h = 0.25 * ((hn + hs) + (he + hw)) - 0.15 * flux
+    new_u = 0.25 * ((un + us) + (ue + uw)) - 0.15 * (u * (ue - uw) + v * (un - us) + (he - hw)) + 0.06 * v
+    new_v = 0.25 * ((vn + vs) + (ve + vw)) - 0.15 * (u * (ve - vw) + v * (vn - vs) + (hn - hs)) - 0.06 * u
+    return new_h, new_u, new_v
+
+
+def halves(x):
+    hi = x.astype(jnp.bfloat16)
+    lo = (x - hi.astype(jnp.float32)).astype(jnp.bfloat16)
+    return hi, lo
+
+
+def left_of(x):
+    return jnp.concatenate(halves(x), axis=1)
+
+
+def right_of(x):
+    wide = jnp.concatenate(halves(x), axis=1)
+    return jnp.concatenate([wide, wide], axis=0)
+
+
+def product(left, right):
+    both = jnp.dot(left, right, preferred_element_type=jnp.float32)
+    half = both.shape[1] // 2
+    return both[:, :half] + both[:, half:]
+
+
+def fused(
+    devices,
+    cores,
+    ens_ref,
+    cell_ref,
+    value_ref,
+    rinv_ref,
+    live_ref,
+    out_ref,
+    send,
+    recv,
+    back_send,
+    back_recv,
+    sems,
+):
+    members = devices * 4
+    me = lax.axis_index("member") * cores + lax.axis_index("group")
+
+    def device_of(k):
+        target = lax.rem(me + k, devices)
+        return target, {"member": target // cores, "group": lax.rem(target, cores)}
+
+    barrier = pltpu.get_barrier_semaphore()
+
+    def greet(i, carry):
+        _, where = device_of(i + 1)
+        pl.semaphore_signal(barrier, inc=1, device_id=where, device_id_type=pl.DeviceIdType.MESH)
+        return carry
+
+    lax.fori_loop(0, devices - 1, greet, 0)
+
+    row = lax.broadcasted_iota(jnp.int32, (8, 128), 0)
+    group = lax.broadcasted_iota(jnp.int32, (8, 128), 1) // 16
+    tiles = ens_ref.shape[3] // 128
+
+    state = []
+    for m in range(0, 4, 2):
+        start = tuple(tuple(ens_ref[m + k, f] for f in range(3)) for k in range(2))
+        state.extend(
+            lax.fori_loop(0, STEPS, lambda _, s: tuple(forecast_step(x) for x in s), start)
+        )
+    for f in range(3):
+        for t in range(tiles):
+            blocks = [
+                swap_groups(state[m][f][:, 128 * t : 128 * t + 128], row, group) for m in range(4)
+            ]
+            for j, block in enumerate(swap_members(blocks, row)):
+                send[8 * t + j, f] = block[0:4]
+                send[8 * t + 4 + j, f] = block[4:8]
+
+    recv[:, pl.ds(me, 1)] = send[me][:, None]
+    pl.semaphore_wait(barrier, devices - 1)
+
+    def scatter(i, carry):
+        target, where = device_of(1 + lax.rem(i + 7, devices - 1))
+        pltpu.make_async_remote_copy(
+            src_ref=send.at[target],
+            dst_ref=recv.at[:, me],
+            send_sem=sems.at[0],
+            recv_sem=sems.at[1],
+            device_id=where,
+            device_id_type=pl.DeviceIdType.MESH,
+        ).start()
+        return carry
+
+    lax.fori_loop(0, devices - 1, scatter, 0)
+
+    cells = 3 * 128
+    picker = (lax.broadcasted_iota(jnp.int32, (cells, 128), 0) == cell_ref[...]).astype(jnp.float32)
+    picker = picker.astype(jnp.bfloat16)
+    obs_row = (lax.rem(cell_ref[...], 128) // PCOL).astype(jnp.float32)
+    dist = (obs_row - 3.5) / 8.0
+    weights = rinv_ref[...] * live_ref[...].astype(jnp.float32) * jnp.exp(-0.5 * dist * dist)
+    square = (members, members)
+    diagonal = lax.broadcasted_iota(jnp.int32, square, 0) == lax.broadcasted_iota(jnp.int32, square, 1)
+
+    arrived = recv.at[:, pl.ds(0, devices - 1)]
+    pltpu.make_async_copy(arrived, arrived, sems.at[1]).wait()
+
+    states = jnp.concatenate([recv[f].reshape(members, 128) for f in range(3)], axis=1)
+    centre = jnp.sum(states, axis=0, keepdims=True) * (1.0 / members)
+    anomaly = states - centre
+    high, low = halves(anomaly)
+    c_high, c_low = halves(centre)
+    c_rest = (centre - c_high.astype(jnp.float32) - c_low.astype(jnp.float32)).astype(jnp.bfloat16)
+    centre_rows = jnp.concatenate([jnp.broadcast_to(c, (16, cells)) for c in (c_high, c_low, c_rest)], axis=0)
+    picked = jnp.dot(
+        jnp.concatenate([high, low, centre_rows], axis=0), picker, preferred_element_type=jnp.float32
+    )
+    seen = picked[:members] + picked[members : 2 * members]
+    at = 2 * members
+    seen_mean = picked[at : at + 1] + picked[at + 16 : at + 17] + picked[at + 32 : at + 33]
+    innov = value_ref[...] - seen_mean
+    weighted = seen * weights
+    pushed = jnp.sum(weighted * innov, axis=1, keepdims=True)
+
+    seen_high, seen_low = halves(seen)
+    right = jnp.concatenate(
+        [
+            jnp.concatenate([seen_high, seen_high], axis=1),
+            jnp.concatenate([seen_low, seen_low], axis=1),
+        ],
+        axis=0,
+    )
+    gram = lax.dot_general(
+        left_of(weighted), right, (((1,), (1,)), ((), ())), preferred_element_type=jnp.float32
+    )
+    system = gram[:, :members] + gram[:, members:] + jnp.where(diagonal, (members - 1) / 1.1, 0.0)
+    norm_c = jnp.max(jnp.sum(jnp.abs(system), axis=0, keepdims=True), axis=1, keepdims=True)
+    root = system / norm_c
+    eye15 = jnp.where(diagonal, 1.5, 0.0)
+    factor = eye15 - 0.5 * root
+    root = product(left_of(root), right_of(factor))
+    inverse = factor
+    for turn in range(1, NS_ITERS - 1):
+        factor = eye15 - 0.5 * product(left_of(inverse), right_of(root))
+        right = right_of(factor)
+        root = product(left_of(root), right)
+        inverse = product(left_of(inverse), right)
+    left = left_of(inverse)
+    last = left_of(eye15 - 0.5 * product(left, right_of(root)))
+    ahead = jnp.concatenate([anomaly, jnp.broadcast_to(pushed, (members, 128))], axis=1)
+    moved = product(last, right_of(product(left, right_of(ahead))))
+    spread = moved[:, :cells]
+    push = moved[:, cells:]
+    scale = math.sqrt(members - 1) * lax.rsqrt(norm_c)
+    for f in range(3):
+        part = spread[:, 128 * f : 128 * f + 128]
+        shift = centre[:, 128 * f : 128 * f + 128] + jnp.sum(part * push, axis=0, keepdims=True) / norm_c
+        back_send[f] = (shift + scale * part).reshape(devices, 4, 128)
+
+    back_recv[pl.ds(me, 1)] = back_send[:, pl.ds(me, 1)].reshape(1, 3, 4, 128)
+
+    def give_back(i, carry):
+        target, where = device_of(1 + lax.rem(i + 7, devices - 1))
+        pltpu.make_async_remote_copy(
+            src_ref=back_send.at[:, target],
+            dst_ref=back_recv.at[me],
+            send_sem=sems.at[2],
+            recv_sem=sems.at[3],
+            device_id=where,
+            device_id_type=pl.DeviceIdType.MESH,
+        ).start()
+        return carry
+
+    lax.fori_loop(0, devices - 1, give_back, 0)
+    sent = send.at[pl.ds(0, devices - 1)]
+    pltpu.make_async_copy(sent, sent, sems.at[0]).wait()
+    arrived = back_recv.at[pl.ds(0, devices - 1)]
+    pltpu.make_async_copy(arrived, arrived, sems.at[3]).wait()
+
+    for f in range(3):
+        for t in range(tiles):
+            blocks = [
+                jnp.concatenate([back_recv[8 * t + j, f], back_recv[8 * t + 4 + j, f]], axis=0)
+                for j in range(4)
+            ]
+            for m, block in enumerate(swap_members(blocks, row)):
+                out_ref[m, f, :, 128 * t : 128 * t + 128] = swap_groups(block, row, group)
+    sent = back_send.at[:, pl.ds(0, devices - 1)]
+    pltpu.make_async_copy(sent, sent, sems.at[2]).wait()
+
+
+def one_strip(ensemble, obs_cell, obs_value, obs_rinv, obs_live):
+    cores = lax.axis_size("group")
+    devices = lax.axis_size("member") * cores
+    vmem = pl.BlockSpec(memory_space=pltpu.VMEM)
+    return pl.pallas_call(
+        functools.partial(fused, devices, cores),
+        out_shape=jax.ShapeDtypeStruct(ensemble.shape, jnp.float32),
+        in_specs=[vmem] * 5,
+        out_specs=vmem,
+        scratch_shapes=[
+            pltpu.VMEM((devices, 3, 4, 128), jnp.float32),
+            pltpu.VMEM((3, devices, 4, 128), jnp.float32),
+            pltpu.VMEM((3, devices, 4, 128), jnp.float32),
+            pltpu.VMEM((devices, 3, 4, 128), jnp.float32),
+            pltpu.SemaphoreType.DMA((4,)),
+        ],
+        compiler_params=pltpu.CompilerParams(collective_id=0, has_side_effects=True),
+        name="fused",
+    )(ensemble, obs_cell[0], obs_value[0], obs_rinv[0], obs_live[0])
+
+
+def fits_one_strip(mesh):
+    return mesh.shape["domain"] == 1
+
+
 def solution(mesh):
     return jax.shard_map(
-        local,
+        one_strip if fits_one_strip(mesh) else local,
         mesh=mesh,
         in_specs=(
             P(("member", "group"), None, "domain", None),

time: 58.6 us -> 27.1 us (0.46)
  Pallas kernels: 0 us -> 25.3 us
  blocking collectives: 11.4 us -> 0 us
  starting transfers between devices: 10.8 us -> 0 us
  local copies, waits for them, and re-layouts: 11.8 us -> 1.62 us
  waiting for transfers between devices: 8.9 us -> 0 us
  matrix products: 7.12 us -> 0 us
  other arithmetic: 6.63 us -> 0 us
  between operations: 1.67 us -> 0.01 us
    pallas_call x0 -> x1, Pallas kernels: none -> 25.3 us  [one_strip(): pl.pallas_call(functools.partial(fused, devices, cores), out_shape=jax.Sh...]
    all_to_all x1 -> x0, blocking collectives: 11.4 us -> none  [local(): lax.all_to_all(result.reshape(ensemble_size, 1, cells), ('member', 'group...]
    all_to_all x1 -> x0, waiting for transfers between devices: 8.89 us -> none  [local(): lax.all_to_all(pieces, ('member', 'group'), split_axis=1, concat_axis=0,...]
    all_to_all x1 -> x0, starting transfers between devices: 7.33 us -> none  [local(): lax.all_to_all(pieces, ('member', 'group'), split_axis=1, concat_axis=0,...]
    dot_general x21 -> x0, matrix products: 7.12 us -> none  [the longest x5 1.99 us: local(): factor = 1.5 * ident - 0.5 * jnp.dot(inverse, root_m, precision=HIGH)]
    slice x66 -> x0, local copies, waits for them, and re-layouts: 6.74 us -> none  [the longest x46 4.09 us: split_parts(): east = jnp.roll(centre, -1, axis=-1)]
    ppermute x5 -> x0, starting transfers between devices: 3.48 us -> none  [the longest x3 2.16 us: with_halo(): lax.ppermute(lax.slice_in_dim(block, block.shape[dim] - width, None, axis...]
    another operation x22 -> x0, other arithmetic: 3.43 us -> none  [advance(): return jnp.stack([new_h, new_u, new_v], axis=1)]
  transfers between devices with their start and end apart: 6 -> 0, of which waited for: 1 -> 0; matrix products, arithmetic and copies ran while one was open for 0% -> 0% of each run, Pallas kernels for 0% -> 0%
where the time goes in v1:
time: 27.1 us; the launch traced here: 26.9 us
  Pallas kernels  25.3 us (93%)
  local copies, waits for them, and re-layouts  1.62 us (6%)
    pallas_call x1, Pallas kernels, one_strip(): pl.pallas_call(functools.partial(fused, devices, cores), out_shape=jax.Sh...  25.3 us
    unnamed x1, local copies, waits for them, and re-layouts  1.62 us

profile of v1, /device:TPU:0, one launch (start us, length us, event | category | flops | bytes accessed | tf_op | source)
XLA Modules:
  0.0 26.9 jit_solution(5519139746670297185)
XLA Ops:
  0.0 25.3 %fused.1 = f32[4,3,8,512]{3,2,1,0:T(8,128)} custom-call(f32[4,3,8,512]{3,2,1,0:T(8,128)} %ens_ref.1, s32[1,128]{1,0:T(1,128)} %bitcast.4, f32[1,128]{1,0:T(1,128)} %bitcast.5, f32[1,128]{1,0:T(1,128)} %bitcast.6, s32[1,128]{1,0:T(1,128)} %bitcast.7), custom_call_target="tpu_custom_call" | custom-call | tf_op jit(solution)/shard_map/fused/pallas_call | solution.py:377
  25.3 1.6 %copy.7 = f32[4,3,8,512]{3,2,1,0:T(8,128)} copy(f32[4,3,8,512]{3,2,1,0:T(8,128)} %fused.1) | data formatting | bytes 393216

commit v2 on v1

--- a/solution.py
+++ b/solution.py
@@ -229,6 +229,33 @@
         target = lax.rem(me + k, devices)
         return target, {"member": target // cores, "group": lax.rem(target, cores)}
 
+    def each_other(send_to):
+        if devices != 32:
+
+            def step(i, carry):
+                send_to(*device_of(i + 1))
+                return carry
+
+            lax.fori_loop(0, devices - 1, step, 0)
+            return
+        plane, seat = me // 8, lax.rem(me, 8)
+        upper = plane // 2
+        order = (
+            3 - 3 * upper,
+            2 - upper,
+            2 * upper + 1 - lax.rem(plane, 2),
+            plane,
+        )
+        for position, there in enumerate(order):
+
+            def step(i, carry):
+                target = there * 8 + lax.rem(seat + i, 8)
+                where = {"member": target // cores, "group": lax.rem(target, cores)}
+                send_to(target, where)
+                return carry
+
+            lax.fori_loop(1 if position == 3 else 0, 8, step, 0)
+
     barrier = pltpu.get_barrier_semaphore()
 
     def greet(i, carry):
@@ -257,22 +284,20 @@
                 send[8 * t + j, f] = block[0:4]
                 send[8 * t + 4 + j, f] = block[4:8]
 
-    recv[:, pl.ds(me, 1)] = send[me][:, None]
+    recv[pl.ds(me, 1)] = send[pl.ds(me, 1)]
     pl.semaphore_wait(barrier, devices - 1)
 
-    def scatter(i, carry):
-        target, where = device_of(1 + lax.rem(i + 7, devices - 1))
+    def scatter(target, where):
         pltpu.make_async_remote_copy(
             src_ref=send.at[target],
-            dst_ref=recv.at[:, me],
+            dst_ref=recv.at[me],
             send_sem=sems.at[0],
             recv_sem=sems.at[1],
             device_id=where,
             device_id_type=pl.DeviceIdType.MESH,
         ).start()
-        return carry
-
-    lax.fori_loop(0, devices - 1, scatter, 0)
+
+    each_other(scatter)
 
     cells = 3 * 128
     picker = (lax.broadcasted_iota(jnp.int32, (cells, 128), 0) == cell_ref[...]).astype(jnp.float32)
@@ -283,10 +308,10 @@
     square = (members, members)
     diagonal = lax.broadcasted_iota(jnp.int32, square, 0) == lax.broadcasted_iota(jnp.int32, square, 1)
 
-    arrived = recv.at[:, pl.ds(0, devices - 1)]
+    arrived = recv.at[pl.ds(0, devices - 1)]
     pltpu.make_async_copy(arrived, arrived, sems.at[1]).wait()
 
-    states = jnp.concatenate([recv[f].reshape(members, 128) for f in range(3)], axis=1)
+    states = jnp.concatenate([recv[:, f].reshape(members, 128) for f in range(3)], axis=1)
     centre = jnp.sum(states, axis=0, keepdims=True) * (1.0 / members)
     anomaly = states - centre
     high, low = halves(anomaly)
@@ -336,59 +361,71 @@
     for f in range(3):
         part = spread[:, 128 * f : 128 * f + 128]
         shift = centre[:, 128 * f : 128 * f + 128] + jnp.sum(part * push, axis=0, keepdims=True) / norm_c
-        back_send[f] = (shift + scale * part).reshape(devices, 4, 128)
-
-    back_recv[pl.ds(me, 1)] = back_send[:, pl.ds(me, 1)].reshape(1, 3, 4, 128)
-
-    def give_back(i, carry):
-        target, where = device_of(1 + lax.rem(i + 7, devices - 1))
+        back_send[:, f] = (shift + scale * part).reshape(devices, 4, 128)
+
+    back_recv[pl.ds(me, 1)] = back_send[pl.ds(me, 1)]
+
+    def give_back(target, where):
         pltpu.make_async_remote_copy(
-            src_ref=back_send.at[:, target],
+            src_ref=back_send.at[target],
             dst_ref=back_recv.at[me],
             send_sem=sems.at[2],
             recv_sem=sems.at[3],
             device_id=where,
             device_id_type=pl.DeviceIdType.MESH,
         ).start()
-        return carry
-
-    lax.fori_loop(0, devices - 1, give_back, 0)
+
+    each_other(give_back)
     sent = send.at[pl.ds(0, devices - 1)]
     pltpu.make_async_copy(sent, sent, sems.at[0]).wait()
     arrived = back_recv.at[pl.ds(0, devices - 1)]
     pltpu.make_async_copy(arrived, arrived, sems.at[3]).wait()
 
+    out_ref[...] = back_recv[...]
+    sent = back_send.at[pl.ds(0, devices - 1)]
+    pltpu.make_async_copy(sent, sent, sems.at[2]).wait()
+
+
+def lay_out(back_ref, out_ref):
+    row = lax.broadcasted_iota(jnp.int32, (8, 128), 0)
+    group = lax.broadcasted_iota(jnp.int32, (8, 128), 1) // 16
+    tiles = out_ref.shape[3] // 128
     for f in range(3):
         for t in range(tiles):
             blocks = [
-                jnp.concatenate([back_recv[8 * t + j, f], back_recv[8 * t + 4 + j, f]], axis=0)
+                jnp.concatenate([back_ref[8 * t + j, f], back_ref[8 * t + 4 + j, f]], axis=0)
                 for j in range(4)
             ]
             for m, block in enumerate(swap_members(blocks, row)):
                 out_ref[m, f, :, 128 * t : 128 * t + 128] = swap_groups(block, row, group)
-    sent = back_send.at[:, pl.ds(0, devices - 1)]
-    pltpu.make_async_copy(sent, sent, sems.at[2]).wait()
 
 
 def one_strip(ensemble, obs_cell, obs_value, obs_rinv, obs_live):
     cores = lax.axis_size("group")
     devices = lax.axis_size("member") * cores
     vmem = pl.BlockSpec(memory_space=pltpu.VMEM)
-    return pl.pallas_call(
+    pieces = pl.pallas_call(
         functools.partial(fused, devices, cores),
-        out_shape=jax.ShapeDtypeStruct(ensemble.shape, jnp.float32),
+        out_shape=pltpu.VMEM((devices, 3, 4, 128), jnp.float32),
         in_specs=[vmem] * 5,
         out_specs=vmem,
         scratch_shapes=[
             pltpu.VMEM((devices, 3, 4, 128), jnp.float32),
-            pltpu.VMEM((3, devices, 4, 128), jnp.float32),
-            pltpu.VMEM((3, devices, 4, 128), jnp.float32),
+            pltpu.VMEM((devices, 3, 4, 128), jnp.float32),
+            pltpu.VMEM((devices, 3, 4, 128), jnp.float32),
             pltpu.VMEM((devices, 3, 4, 128), jnp.float32),
             pltpu.SemaphoreType.DMA((4,)),
         ],
         compiler_params=pltpu.CompilerParams(collective_id=0, has_side_effects=True),
         name="fused",
     )(ensemble, obs_cell[0], obs_value[0], obs_rinv[0], obs_live[0])
+    return pl.pallas_call(
+        lay_out,
+        out_shape=jax.ShapeDtypeStruct(ensemble.shape, jnp.float32),
+        in_specs=[vmem],
+        out_specs=vmem,
+        name="lay_out",
+    )(pltpu.with_memory_space_constraint(pieces, pltpu.VMEM))
 
 
 def fits_one_strip(mesh):

time: 27.1 us -> 24.4 us (0.900)
  local copies, waits for them, and re-layouts: 1.62 us -> 0 us
  Pallas kernels: 25.3 us -> 24.3 us
    unnamed x1 -> x0, local copies, waits for them, and re-layouts: 1.62 us -> none
    pallas_call x1 -> x2, Pallas kernels: 25.3 us -> 24.3 us  [the longest x1 23 us: one_strip(): pl.pallas_call(functools.partial(fused, devices, cores), out_shape=pltpu....]
where the time goes in v2:
time: 24.4 us; the launch traced here: 24.3 us
  Pallas kernels  24.3 us (100%)
    pallas_call x1, Pallas kernels, one_strip(): pl.pallas_call(functools.partial(fused, devices, cores), out_shape=pltpu....  23 us
    pallas_call x1, Pallas kernels, one_strip(): pl.pallas_call(lay_out, out_shape=jax.ShapeDtypeStruct(ensemble.shape, jn...  1.29 us

profile of v2, /device:TPU:0, one launch (start us, length us, event | category | flops | bytes accessed | tf_op | source)
XLA Modules:
  0.0 24.3 jit_solution(14911496882281874776)
XLA Ops:
  0.0 23.0 %fused.1.back_ref = f32[32,3,4,128]{3,2,1,0:T(4,128)S(1)} custom-call(f32[4,3,8,512]{3,2,1,0:T(8,128)} %ens_ref.1, s32[1,128]{1,0:T(1,128)} %bitcast.4, f32[1,128]{1,0:T(1,128)} %bitcast.5, f32[1,128]{1,0:T(1,128)} %bitcast.6, s32[1,128]{1,0:T(1,128)} %bitcast.7), custom_call_target="tpu_custom_call" | custom-call | tf_op jit(solution)/shard_map/fused/pallas_call | solution.py:407
  23.0 1.3 %lay_out.1 = f32[4,3,8,512]{3,2,1,0:T(8,128)} custom-call(f32[32,3,4,128]{3,2,1,0:T(4,128)S(1)} %fused.1.back_ref), custom_call_target="tpu_custom_call" | custom-call | tf_op jit(solution)/shard_map/lay_out/pallas_call | solution.py:422

commit v3 on v2

--- a/solution.py
+++ b/solution.py
@@ -210,12 +210,18 @@
 def fused(
     devices,
     cores,
+    ens_hbm,
+    cell_hbm,
+    value_hbm,
+    rinv_hbm,
+    live_hbm,
+    out_ref,
     ens_ref,
     cell_ref,
     value_ref,
     rinv_ref,
     live_ref,
-    out_ref,
+    load_sems,
     send,
     recv,
     back_send,
@@ -256,6 +262,17 @@
 
             lax.fori_loop(1 if position == 3 else 0, 8, step, 0)
 
+    pairs = (
+        (ens_hbm, ens_ref),
+        (cell_hbm, cell_ref),
+        (value_hbm, value_ref),
+        (rinv_hbm, rinv_ref),
+        (live_hbm, live_ref),
+    )
+    loads = [pltpu.make_async_copy(a, b, load_sems.at[i]) for i, (a, b) in enumerate(pairs)]
+    for load in loads:
+        load.start()
+
     barrier = pltpu.get_barrier_semaphore()
 
     def greet(i, carry):
@@ -264,6 +281,7 @@
         return carry
 
     lax.fori_loop(0, devices - 1, greet, 0)
+    loads[0].wait()
 
     row = lax.broadcasted_iota(jnp.int32, (8, 128), 0)
     group = lax.broadcasted_iota(jnp.int32, (8, 128), 1) // 16
@@ -299,6 +317,8 @@
 
     each_other(scatter)
 
+    for load in loads[1:]:
+        load.wait()
     cells = 3 * 128
     picker = (lax.broadcasted_iota(jnp.int32, (cells, 128), 0) == cell_ref[...]).astype(jnp.float32)
     picker = picker.astype(jnp.bfloat16)
@@ -407,9 +427,15 @@
     pieces = pl.pallas_call(
         functools.partial(fused, devices, cores),
         out_shape=pltpu.VMEM((devices, 3, 4, 128), jnp.float32),
-        in_specs=[vmem] * 5,
+        in_specs=[pl.BlockSpec(memory_space=pltpu.HBM)] * 5,
         out_specs=vmem,
         scratch_shapes=[
+            pltpu.VMEM(ensemble.shape, jnp.float32),
+            pltpu.VMEM(obs_cell.shape[1:], jnp.int32),
+            pltpu.VMEM(obs_value.shape[1:], jnp.float32),
+            pltpu.VMEM(obs_rinv.shape[1:], jnp.float32),
+            pltpu.VMEM(obs_live.shape[1:], jnp.int32),
+            pltpu.SemaphoreType.DMA((5,)),
             pltpu.VMEM((devices, 3, 4, 128), jnp.float32),
             pltpu.VMEM((devices, 3, 4, 128), jnp.float32),
             pltpu.VMEM((devices, 3, 4, 128), jnp.float32),

time: 24.4 us -> 23.6 us (0.967)
  Pallas kernels: 24.3 us -> 23.5 us
    pallas_call x1, Pallas kernels: 23 us -> 22.2 us  [one_strip(): pl.pallas_call(functools.partial(fused, devices, cores), out_shape=pltpu....]
where the time goes in v3:
time: 23.6 us; the launch traced here: 23.5 us
  Pallas kernels  23.5 us (100%)
    pallas_call x1, Pallas kernels, one_strip(): pl.pallas_call(functools.partial(fused, devices, cores), out_shape=pltpu....  22.2 us
    pallas_call x1, Pallas kernels, one_strip(): pl.pallas_call(lay_out, out_shape=jax.ShapeDtypeStruct(ensemble.shape, jn...  1.29 us

profile of v3, /device:TPU:0, one launch (start us, length us, event | category | flops | bytes accessed | tf_op | source)
XLA Modules:
  0.0 23.5 jit_solution(13099438855122160512)
XLA Ops:
  0.0 22.2 %fused.1.back_ref = f32[32,3,4,128]{3,2,1,0:T(4,128)S(1)} custom-call(f32[4,3,8,512]{3,2,1,0:T(8,128)} %ens_hbm.1, s32[1,128]{1,0:T(1,128)} %bitcast.4, f32[1,128]{1,0:T(1,128)} %bitcast.5, f32[1,128]{1,0:T(1,128)} %bitcast.6, s32[1,128]{1,0:T(1,128)} %bitcast.7), custom_call_target="tpu_custom_call" | custom-call | tf_op jit(solution)/shard_map/fused/pallas_call | solution.py:427
  22.2 1.3 %lay_out.1 = f32[4,3,8,512]{3,2,1,0:T(8,128)} custom-call(f32[32,3,4,128]{3,2,1,0:T(4,128)S(1)} %fused.1.back_ref), custom_call_target="tpu_custom_call" | custom-call | tf_op jit(solution)/shard_map/lay_out/pallas_call | solution.py:448
